TPU v7x, 256 devices: a whole 4x4x8 slice. The times are simulated.
256 devices in a mesh: site: 2 (over core), wide: 32 (over x, z), narrow: 4 (over y).
Axes of the slice: x: 4, y: 4, z: 8, core: 2. Of those that a mesh axis runs over, the one named last changes fastest.
Arguments:
- initial_rows: float32 [64, 4, 2048], P('site', 'narrow'), may hold values from -6 to 6
- outcomes: int32 [64, 4], replicated, may hold values 0 or 1
- tensors: float32 [4, 2, 4, 2048, 8192], P('site', None, 'narrow', None, 'wide'), may hold values from -0.25 to 0.25
Outputs:
- final_rows: float32 [64, 4, 2048], P('site', 'narrow')
- log_weight: float32 [64], P('site')
All inputs are finite; a program needn't handle non-finite values.
Results may differ from a plain program's by a relative error of at most 0.0003.
Values sent between devices are 32-bit elements; how exact they have to be, the bound alone decides.
A program may use at most 64 MiB of HBM per device.

v0:
```python
import jax
import jax.numpy as jnp
from jax import lax
from jax.sharding import PartitionSpec as P

BOND = 8192
epsilon = 1e-06
highest = lax.Precision.HIGHEST


def from_partner(value, axis, distance):
    mask = 2**distance
    pairs = [(source, source ^ mask) for source in range(lax.axis_size(axis))]
    return lax.ppermute(value, axis, pairs)


def advance(held, log_sum, site_tensor, chosen):
    front = held.shape[0]
    groups = lax.axis_size("narrow")
    share = front // groups
    summed = lax.psum_scatter(
        jnp.einsum(
            "bar,oard->bod",
            held,
            site_tensor,
            precision=highest,
            preferred_element_type=jnp.float32,
        ),
        "narrow",
        scatter_dimension=0,
        tiled=True,
    )
    local_choice = lax.dynamic_slice_in_dim(chosen, lax.axis_index("narrow") * share, share, 0)
    squares = jnp.sum(summed * summed, axis=2)
    raw_kept = jnp.where(local_choice[:, None] == 0, summed[:, 0, :], summed[:, 1, :])
    totals = lax.psum(squares, "wide")
    both_mean = (totals[:, 0] + totals[:, 1]) / (2.0 * BOND)
    scale = lax.rsqrt(both_mean + epsilon)
    full_rows = lax.all_gather(raw_kept * scale[:, None], "wide", axis=1, tiled=True)
    kept_square = jnp.where(local_choice == 0, totals[:, 0], totals[:, 1])
    local_ratio = jnp.log(kept_square / BOND + epsilon) - jnp.log(both_mean + epsilon)
    ratio_table = jnp.broadcast_to(local_ratio[:, None], (share, groups))
    split_rows = full_rows.reshape(share, groups, -1)
    moved, moved_ratio = (
        lax.all_to_all(split_rows, "narrow", split_axis=1, concat_axis=0, tiled=True),
        lax.all_to_all(ratio_table, "narrow", split_axis=1, concat_axis=0, tiled=True),
    )
    return (moved, log_sum + moved_ratio[:, 0])


def run_section(held, log_sum, tensors, chosen_block):
    for local_site in range(tensors.shape[0]):
        held, log_sum = advance(held, log_sum, tensors[local_site], chosen_block[:, local_site])
    return (held, log_sum)


def hand_over(held, log_sum):
    moved_rows, moved_sum = from_partner((held, log_sum), "site", 0)
    return (moved_rows, moved_sum)


def shards(initial_rows, outcomes, tensors):
    section = lax.axis_index("site")
    front = initial_rows.shape[0]
    local_count = tensors.shape[0]
    section_columns = lax.dynamic_slice_in_dim(outcomes, section * local_count, local_count, 1)
    held = initial_rows
    log_sum = jnp.zeros((front,), jnp.float32)
    front_order = (section, 1 - section, section)
    for turn_index in range(3):
        new_rows, new_sum = run_section(
            held,
            log_sum,
            tensors,
            lax.dynamic_slice_in_dim(section_columns, front_order[turn_index] * front, front, 0),
        )
        if turn_index == 1:
            held, log_sum = (new_rows, new_sum)
        else:
            active = section == 0 if turn_index == 0 else section == 1
            held = jnp.where(active, new_rows, held)
            log_sum = jnp.where(active, new_sum, log_sum)
        if turn_index < 2:
            held, log_sum = hand_over(held, log_sum)
    return (held, log_sum)


def solution(mesh):
    placed = (P("site", "narrow", None), P(), P("site", None, "narrow", None, "wide"))
    return jax.shard_map(
        shards,
        mesh=mesh,
        in_specs=placed,
        out_specs=(P("site", "narrow", None), P("site")),
        check_vma=False,
    )
```

profile of v0, /device:TPU:2, one launch (start us, length us, event | category | flops | bytes accessed | tf_op | source)
XLA Modules:
  0.0 993.4 jit_solution(1777501969221541964)
XLA Ops:
  7.2 5.4 fusion.2
  13.6 25.4 %reduce-scatter.7.cloned.1.call-done = f32[8,2,256]{2,0,1:T(8,128)} async-done(((f32[32,2,256]{2,0,1:T(8,128)}), f32[8,2,256]{2,0,1:T(8,128)}) %reduce-scatter.7.cloned.1.call-update) | async-done | bytes 16400 | tf_op jit(solution)/shard_map/reduce_scatter | solution.py:21
  39.8 63.2 %psum.42 = f32[8,2]{0,1:T(2,128)S(1)} all-reduce(f32[8,2]{0,1:T(2,128)S(1)} %multiply_reduce_fusion.5), channel_id=1, replica_groups=mesh['site'=2,'wide'=32,'narrow'=4] {'wide'}, use_global_device_ids=true, to_apply=%region_2.3 | all-reduce | flops 16 | bytes 128 | tf_op jit(solution)/shard_map/psum | solution.py:36
  103.9 58.4 %all_gather.18 = f32[8,8192]{1,0:T(8,128)S(1)} all-gather(f32[8,256]{1,0:T(8,128)S(1)} %fusion.24), channel_id=1, replica_groups=mesh['site'=2,'wide'=32,'narrow'=4] {'wide'}, dimensions={1}, use_global_device_ids=true | all-gather | bytes 270336 | tf_op jit(solution)/shard_map/all_gather | solution.py:39
  162.3 9.2 all_to_all.171
  171.5 5.3 fusion.5
  176.9 18.2 %reduce-scatter.9.cloned.1.call-done = f32[8,2,256]{2,0,1:T(8,128)} async-done(((f32[32,2,256]{2,0,1:T(8,128)}), f32[8,2,256]{2,0,1:T(8,128)}) %reduce-scatter.9.cloned.1.call-update) | async-done | bytes 16400 | tf_op jit(solution)/shard_map/reduce_scatter | solution.py:21
  195.9 63.2 %psum.43 = f32[8,2]{0,1:T(2,128)S(1)} all-reduce(f32[8,2]{0,1:T(2,128)S(1)} %multiply_reduce_fusion.4), channel_id=1, replica_groups=mesh['site'=2,'wide'=32,'narrow'=4] {'wide'}, use_global_device_ids=true, to_apply=%region_5.6 | all-reduce | flops 16 | bytes 128 | tf_op jit(solution)/shard_map/psum | solution.py:36
  260.0 62.4 %all_gather.19 = f32[8,8192]{1,0:T(8,128)} all-gather(f32[8,256]{1,0:T(8,128)S(1)} %fusion.22), channel_id=1, replica_groups=mesh['site'=2,'wide'=32,'narrow'=4] {'wide'}, dimensions={1}, use_global_device_ids=true | all-gather | bytes 270336 | tf_op jit(solution)/shard_map/all_gather | solution.py:39
  325.9 6.6 all-to-all-done.1
  334.2 5.3 fusion.1
  339.6 18.2 %reduce-scatter.11.cloned.1.call-done = f32[8,2,256]{2,0,1:T(8,128)} async-done(((f32[32,2,256]{2,0,1:T(8,128)}), f32[8,2,256]{2,0,1:T(8,128)}) %reduce-scatter.11.cloned.1.call-update) | async-done | bytes 16400 | tf_op jit(solution)/shard_map/reduce_scatter | solution.py:21
  358.6 63.2 %psum.44 = f32[8,2]{0,1:T(2,128)S(1)} all-reduce(f32[8,2]{0,1:T(2,128)S(1)} %multiply_reduce_fusion.3), channel_id=1, replica_groups=mesh['site'=2,'wide'=32,'narrow'=4] {'wide'}, use_global_device_ids=true, to_apply=%region_8.9 | all-reduce | flops 16 | bytes 128 | tf_op jit(solution)/shard_map/psum | solution.py:36
  422.8 58.4 %all_gather.20 = f32[8,8192]{1,0:T(8,128)S(1)} all-gather(f32[8,256]{1,0:T(8,128)S(1)} %fusion.20), channel_id=1, replica_groups=mesh['site'=2,'wide'=32,'narrow'=4] {'wide'}, dimensions={1}, use_global_device_ids=true | all-gather | bytes 270336 | tf_op jit(solution)/shard_map/all_gather | solution.py:39
  481.1 9.2 all_to_all.172
  490.3 5.3 fusion.4
  495.7 18.1 %reduce-scatter.13.cloned.1.call-done = f32[8,2,256]{2,0,1:T(8,128)} async-done(((f32[32,2,256]{2,0,1:T(8,128)}), f32[8,2,256]{2,0,1:T(8,128)}) %reduce-scatter.13.cloned.1.call-update) | async-done | bytes 16400 | tf_op jit(solution)/shard_map/reduce_scatter | solution.py:21
  514.7 63.2 %psum.45 = f32[8,2]{0,1:T(2,128)S(1)} all-reduce(f32[8,2]{0,1:T(2,128)S(1)} %multiply_reduce_fusion.2), channel_id=1, replica_groups=mesh['site'=2,'wide'=32,'narrow'=4] {'wide'}, use_global_device_ids=true, to_apply=%region_11.12 | all-reduce | flops 16 | bytes 128 | tf_op jit(solution)/shard_map/psum | solution.py:36
  578.8 58.4 %all_gather.21 = f32[8,8192]{1,0:T(8,128)S(1)} all-gather(f32[8,256]{1,0:T(8,128)S(1)} %fusion.18), channel_id=1, replica_groups=mesh['site'=2,'wide'=32,'narrow'=4] {'wide'}, dimensions={1}, use_global_device_ids=true | all-gather | bytes 270336 | tf_op jit(solution)/shard_map/all_gather | solution.py:39
  637.2 9.2 all_to_all.173
  647.9 5.3 fusion
  653.3 7.6 all_to_all.174
  664.6 5.2 all-to-all-done.7
  676.0 63.3 %psum.46 = f32[8,2]{0,1:T(2,128)S(1)} all-reduce(f32[8,2]{0,1:T(2,128)S(1)} %multiply_reduce_fusion.1), channel_id=1, replica_groups=mesh['site'=2,'wide'=32,'narrow'=4] {'wide'}, use_global_device_ids=true, to_apply=%region_14.15 | all-reduce | flops 16 | bytes 128 | tf_op jit(solution)/shard_map/psum | solution.py:36
  745.5 62.4 %all_gather.22 = f32[8,8192]{1,0:T(8,128)} all-gather(f32[8,256]{1,0:T(8,128)S(1)} %fusion.16), channel_id=1, replica_groups=mesh['site'=2,'wide'=32,'narrow'=4] {'wide'}, dimensions={1}, use_global_device_ids=true | all-gather | bytes 270336 | tf_op jit(solution)/shard_map/all_gather | solution.py:39
  812.9 6.5 all-to-all-done.4
  819.4 5.3 fusion.3
  828.6 5.1 all-to-all-done.10
  833.7 9.2 reduce-scatter.17.cloned.1.call-done
  843.8 63.2 %psum.47 = f32[8,2]{0,1:T(2,128)S(1)} all-reduce(f32[8,2]{0,1:T(2,128)S(1)} %multiply_reduce_fusion), channel_id=1, replica_groups=mesh['site'=2,'wide'=32,'narrow'=4] {'wide'}, use_global_device_ids=true, to_apply=%region_17.18 | all-reduce | flops 16 | bytes 128 | tf_op jit(solution)/shard_map/psum | solution.py:36
  911.7 62.4 %all_gather.23 = f32[8,8192]{1,0:T(8,128)} all-gather(f32[8,256]{1,0:T(8,128)S(1)} %fusion.14), channel_id=1, replica_groups=mesh['site'=2,'wide'=32,'narrow'=4] {'wide'}, dimensions={1}, use_global_device_ids=true | all-gather | bytes 270336 | tf_op jit(solution)/shard_map/all_gather | solution.py:39
  979.5 6.1 all-to-all-done.5
  (80 shorter events, 51.7 us)
Async XLA Ops:
  7.2 325.3 %copy-start = (f32[32,1,2048]{2,1,0:T(1,128)S(1)}, f32[32,1,2048]{2,1,0:T(1,128)}, u32[]{:S(2)}) copy-start(f32[32,1,2048]{2,1,0:T(1,128)} %param.3) | copy-start | bytes 786436
  7.2 31.8 %reduce-scatter.7.cloned.1.call-start = ((), (), s32[]{:S(2)}) async-start(), calls=%async_computation.18 | async-start | bytes 81920 | tf_op jit(solution)/shard_map/reduce_scatter | solution.py:21
  12.7 182.3 %reduce-scatter.9.cloned.1.call-start = ((), (), s32[]{:S(2)}) async-start(), calls=%async_computation.19 | async-start | bytes 81920 | tf_op jit(solution)/shard_map/reduce_scatter | solution.py:21
  322.4 10.1 %all-to-all-start.1 = ((f32[8,4,2048]{2,0,1:T(8,128)}), f32[8,4,2048]{2,0,1:T(8,128)S(1)}, u32[]{:S(2)}, u32[]{:S(2)}) async-start(f32[8,4,2048]{2,0,1:T(8,128)} %bitcast.19), calls=%async_computation.3 | async-start | bytes 524288 | tf_op jit(solution)/shard_map/all_to_all | solution.py:45
  325.8 31.9 %reduce-scatter.11.cloned.1.call-start = ((), (), s32[]{:S(2)}) async-start(), calls=%async_computation.20 | async-start | bytes 81920 | tf_op jit(solution)/shard_map/reduce_scatter | solution.py:21
  332.6 1.6 collective-permute-start
  339.5 174.3 %reduce-scatter.13.cloned.1.call-start = ((), (), s32[]{:S(2)}) async-start(), calls=%async_computation.21 | async-start | bytes 81920 | tf_op jit(solution)/shard_map/reduce_scatter | solution.py:21
  495.6 175.8 %reduce-scatter.15.cloned.1.call-start = ((), (), s32[]{:S(2)}) async-start(), calls=%async_computation.22 | async-start | bytes 81920 | tf_op jit(solution)/shard_map/reduce_scatter | solution.py:21
  646.4 1.5 collective-permute-start.1
  661.5 8.4 all-to-all-start.7
  670.0 154.7 %collective-permute-start.2 = (f32[32]{0:T(128)S(1)}, f32[32]{0:T(128)S(1)}, u32[]{:S(2)}, u32[]{:S(2)}) collective-permute-start(f32[32]{0:T(128)S(1)} %select_n.125), channel_id=1, source_target_pairs={{0,128},{128,0},{1,129},{129,1},{2,130},{130,2},{3,131},{131,3},{4... | collective-permute-start | bytes 392 | tf_op jit(solution)/shard_map/ppermute | solution.py:14
  672.8 67.4 %all-to-all-start.8 = ((f32[8,4,1]{0,2,1:T(1,128)}), f32[8,4,1]{0,2,1:T(1,128)S(1)}, u32[]{:S(2)}, u32[]{:S(2)}) async-start(f32[8,4,1]{0,2,1:T(1,128)} %broadcast_in_dim.99), calls=%async_computation.14 | async-start | bytes 4096 | tf_op jit(solution)/shard_map/all_to_all | solution.py:46
  740.7 67.1 %all-to-all-start.9 = ((f32[8,4,1]{0,2,1:T(1,128)}), f32[8,4,1]{0,2,1:T(1,128)S(1)}, u32[]{:S(2)}, u32[]{:S(2)}) async-start(f32[8,4,1]{0,2,1:T(1,128)} %broadcast_in_dim.100), calls=%async_computation.15 | async-start | bytes 4096 | tf_op jit(solution)/shard_map/all_to_all | solution.py:46
  807.9 11.5 %all-to-all-start.4 = ((f32[8,4,2048]{2,0,1:T(8,128)}), f32[8,4,2048]{2,0,1:T(8,128)S(1)}, u32[]{:S(2)}, u32[]{:S(2)}) async-start(f32[8,4,2048]{2,0,1:T(8,128)} %bitcast.45), calls=%async_computation.9 | async-start | bytes 524288 | tf_op jit(solution)/shard_map/all_to_all | solution.py:45
  812.7 30.3 %reduce-scatter.17.cloned.1.call-start = ((), (), s32[]{:S(2)}) async-start(), calls=%async_computation.23 | async-start | bytes 81920 | tf_op jit(solution)/shard_map/reduce_scatter | solution.py:21
  825.3 8.4 all-to-all-start.10
  828.5 150.6 %collective-permute-start.3 = (f32[32]{0:T(128)S(1)}, f32[32]{0:T(128)S(1)}, u32[]{:S(2)}, u32[]{:S(2)}) collective-permute-start(f32[32]{0:T(128)S(1)} %add_add_fusion), channel_id=1, source_target_pairs={{0,128},{128,0},{1,129},{129,1},{2,130},{130,2},{3,131},{131,3},{4... | collective-permute-start | bytes 392 | tf_op jit(solution)/shard_map/ppermute | solution.py:14
  907.7 66.4 %all-to-all-start.11 = ((f32[8,4,1]{0,2,1:T(1,128)}), f32[8,4,1]{0,2,1:T(1,128)S(1)}, u32[]{:S(2)}, u32[]{:S(2)}) async-start(f32[8,4,1]{0,2,1:T(1,128)} %broadcast_in_dim.102), calls=%async_computation.17 | async-start | bytes 4096 | tf_op jit(solution)/shard_map/all_to_all | solution.py:46
  974.1 11.4 %all-to-all-start.5 = ((f32[8,4,2048]{2,0,1:T(8,128)}), f32[8,4,2048]{2,0,1:T(8,128)S(1)}, u32[]{:S(2)}, u32[]{:S(2)}) async-start(f32[8,4,2048]{2,0,1:T(8,128)} %bitcast.53), calls=%async_computation.11 | async-start | bytes 524288 | tf_op jit(solution)/shard_map/all_to_all | solution.py:45
Sparse Core Ops, SparseCore 0:
  12.8 26.1 reduce-scatter.6
  177.0 18.0 reduce-scatter.8
  339.6 18.0 reduce-scatter.10
  495.8 18.0 reduce-scatter.12
  653.4 18.0 reduce-scatter.14
  824.8 18.0 reduce-scatter.16
where the time goes:
time: 995 us; the launch traced here: 993 us
  blocking collectives  777 us (78%)
  waiting for transfers between devices  123 us (12%)
  matrix products  31.9 us (3%)
  starting transfers between devices  30.9 us (3%)
  between operations  14.3 us (1%)
  other arithmetic  11 us (1%)
    psum x6, blocking collectives, advance(): totals = lax.psum(squares, 'wide')  379 us
    all_gather x6, blocking collectives, advance(): lax.all_gather(raw_kept * scale[:, None], 'wide', axis=1, tiled=True)  362 us
    reduce_scatter x6, waiting for transfers between devices, advance(): lax.psum_scatter(jnp.einsum('bar,oard->bod', held, site_tensor, precision...  90.4 us
    dot_general x6, matrix products, advance(): jnp.einsum('bar,oard->bod', held, site_tensor, precision=highest, preferr...  31.9 us
    all_to_all x3, blocking collectives, advance(): lax.all_to_all(split_rows, 'narrow', split_axis=1, concat_axis=0, tiled=T...  27.6 us
  transfers between devices with their start and end apart: 18, of which 13 were waited for; matrix products, arithmetic and copies ran while one was open for 1% of the time, Pallas kernels for 0%

commit v1 on v0

--- a/solution.py
+++ b/solution.py
@@ -36,7 +36,12 @@
     totals = lax.psum(squares, "wide")
     both_mean = (totals[:, 0] + totals[:, 1]) / (2.0 * BOND)
     scale = lax.rsqrt(both_mean + epsilon)
-    full_rows = lax.all_gather(raw_kept * scale[:, None], "wide", axis=1, tiled=True)
+    full_rows = jnp.concatenate(
+        lax.all_to_all(
+            jnp.stack([raw_kept * scale[:, None]] * lax.axis_size("wide")), "wide", 0, 0
+        ),
+        axis=1,
+    )
     kept_square = jnp.where(local_choice == 0, totals[:, 0], totals[:, 1])
     local_ratio = jnp.log(kept_square / BOND + epsilon) - jnp.log(both_mean + epsilon)
     ratio_table = jnp.broadcast_to(local_ratio[:, None], (share, groups))

time: 995 us -> 804 us (0.81)
  blocking collectives: 777 us -> 532 us
  waiting for transfers between devices: 123 us -> 157 us
  starting transfers between devices: 30.9 us -> 48.1 us
    all_gather x6 -> x0, blocking collectives: 362 us -> none  [advance(): lax.all_gather(raw_kept * scale[:, None], 'wide', axis=1, tiled=True)]
    all_to_all x1 -> x5, blocking collectives: 7.62 us -> 125 us  [advance(): lax.all_to_all(jnp.stack([raw_kept * scale[:, None]] * lax.axis_size('wid...]
    all_to_all x0 -> x1, starting transfers between devices: none -> 16.6 us  [advance(): lax.all_to_all(jnp.stack([raw_kept * scale[:, None]] * lax.axis_size('wid...]
    reduce_scatter x6, waiting for transfers between devices: 90.4 us -> 105 us  [advance(): lax.psum_scatter(jnp.einsum('bar,oard->bod', held, site_tensor, precision...]
    all_to_all x5 -> x6, starting transfers between devices: 17.5 us -> 20.8 us  [advance(): lax.all_to_all(ratio_table, 'narrow', split_axis=1, concat_axis=0, tiled=...]
  transfers between devices with their start and end apart: 18 -> 20, of which waited for: 13 -> 16; matrix products, arithmetic and copies ran while one was open for 1% -> 1% of each run, Pallas kernels for 0% -> 0%
where the time goes in v1:
time: 804 us; the launch traced here: 801 us
  blocking collectives  532 us (66%)
  waiting for transfers between devices  157 us (20%)
  starting transfers between devices  48.1 us (6%)
  matrix products  31.9 us (4%)
  between operations  14.3 us (2%)
  other arithmetic  11 us (1%)
    psum x6, blocking collectives, advance(): totals = lax.psum(squares, 'wide')  379 us
    all_to_all x5, blocking collectives, advance(): lax.all_to_all(jnp.stack([raw_kept * scale[:, None]] * lax.axis_size('wid...  125 us
    reduce_scatter x6, waiting for transfers between devices, advance(): lax.psum_scatter(jnp.einsum('bar,oard->bod', held, site_tensor, precision...  105 us
    dot_general x6, matrix products, advance(): jnp.einsum('bar,oard->bod', held, site_tensor, precision=highest, preferr...  31.9 us
    all_to_all x3, blocking collectives, advance(): lax.all_to_all(split_rows, 'narrow', split_axis=1, concat_axis=0, tiled=T...  27.6 us
    all_to_all x6, starting transfers between devices, advance(): lax.all_to_all(ratio_table, 'narrow', split_axis=1, concat_axis=0, tiled=...  20.8 us
    all_to_all x3, waiting for transfers between devices, advance(): lax.all_to_all(split_rows, 'narrow', split_axis=1, concat_axis=0, tiled=T...  19.4 us
    all_to_all x6, waiting for transfers between devices, advance(): lax.all_to_all(ratio_table, 'narrow', split_axis=1, concat_axis=0, tiled=...  19.4 us
  transfers between devices with their start and end apart: 20, of which 16 were waited for; matrix products, arithmetic and copies ran while one was open for 1% of the time, Pallas kernels for 0%

profile of v1, /device:TPU:2, one launch (start us, length us, event | category | flops | bytes accessed | tf_op | source)
XLA Modules:
  0.0 801.0 jit_solution(17320977020725761283)
XLA Ops:
  7.2 5.4 fusion.2
  13.6 25.4 %reduce-scatter.7.cloned.1.call-done = f32[8,2,256]{2,0,1:T(8,128)} async-done(((f32[32,2,256]{2,0,1:T(8,128)}), f32[8,2,256]{2,0,1:T(8,128)}) %reduce-scatter.7.cloned.1.call-update) | async-done | bytes 16400 | tf_op jit(solution)/shard_map/reduce_scatter | solution.py:21
  39.8 63.2 %psum.42 = f32[8,2]{0,1:T(2,128)S(1)} all-reduce(f32[8,2]{0,1:T(2,128)S(1)} %multiply_reduce_fusion.5), channel_id=1, replica_groups=mesh['site'=2,'wide'=32,'narrow'=4] {'wide'}, use_global_device_ids=true, to_apply=%region_2.3 | all-reduce | flops 16 | bytes 128 | tf_op jit(solution)/shard_map/psum | solution.py:36
  104.0 24.8 %all_to_all.201 = f32[32,8,256]{2,1,0:T(8,128)S(1)} all-to-all(f32[32,8,256]{2,1,0:T(8,128)S(1)} %stack.12), channel_id=1, replica_groups=mesh['site'=2,'wide'=32,'narrow'=4] {'wide'}, dimensions={0} | all-to-all | bytes 524288 | tf_op jit(solution)/shard_map/all_to_all | solution.py:40
  128.7 9.2 %all_to_all.202 = f32[8,4,2048]{2,0,1:T(8,128)S(1)} all-to-all(f32[8,4,2048]{2,0,1:T(8,128)S(1)} %bitcast.195), channel_id=1, replica_groups=mesh['site'=2,'wide'=32,'narrow'=4] {'narrow'}, dimensions={1} | all-to-all | bytes 524288 | tf_op jit(solution)/shard_map/all_to_all | solution.py:50
  137.9 5.3 fusion.5
  143.3 18.4 %reduce-scatter.9.cloned.1.call-done = f32[8,2,256]{2,0,1:T(8,128)} async-done(((f32[32,2,256]{2,0,1:T(8,128)}), f32[8,2,256]{2,0,1:T(8,128)}) %reduce-scatter.9.cloned.1.call-update) | async-done | bytes 16400 | tf_op jit(solution)/shard_map/reduce_scatter | solution.py:21
  162.6 63.2 %psum.43 = f32[8,2]{0,1:T(2,128)S(1)} all-reduce(f32[8,2]{0,1:T(2,128)S(1)} %multiply_reduce_fusion.4), channel_id=1, replica_groups=mesh['site'=2,'wide'=32,'narrow'=4] {'wide'}, use_global_device_ids=true, to_apply=%region_5.6 | all-reduce | flops 16 | bytes 128 | tf_op jit(solution)/shard_map/psum | solution.py:36
  226.7 25.5 %all_to_all.203 = f32[32,8,256]{2,1,0:T(8,128)} all-to-all(f32[32,8,256]{2,1,0:T(8,128)S(1)} %stack.13), channel_id=1, replica_groups=mesh['site'=2,'wide'=32,'narrow'=4] {'wide'}, dimensions={0} | all-to-all | bytes 524288 | tf_op jit(solution)/shard_map/all_to_all | solution.py:40
  255.7 6.6 all-to-all-done.3
  264.0 5.3 fusion.1
  269.4 18.4 %reduce-scatter.11.cloned.1.call-done = f32[8,2,256]{2,0,1:T(8,128)} async-done(((f32[32,2,256]{2,0,1:T(8,128)}), f32[8,2,256]{2,0,1:T(8,128)}) %reduce-scatter.11.cloned.1.call-update) | async-done | bytes 16400 | tf_op jit(solution)/shard_map/reduce_scatter | solution.py:21
  288.6 63.2 %psum.44 = f32[8,2]{0,1:T(2,128)S(1)} all-reduce(f32[8,2]{0,1:T(2,128)S(1)} %multiply_reduce_fusion.3), channel_id=1, replica_groups=mesh['site'=2,'wide'=32,'narrow'=4] {'wide'}, use_global_device_ids=true, to_apply=%region_8.9 | all-reduce | flops 16 | bytes 128 | tf_op jit(solution)/shard_map/psum | solution.py:36
  352.7 24.8 %all_to_all.204 = f32[32,8,256]{2,1,0:T(8,128)S(1)} all-to-all(f32[32,8,256]{2,1,0:T(8,128)S(1)} %stack.14), channel_id=1, replica_groups=mesh['site'=2,'wide'=32,'narrow'=4] {'wide'}, dimensions={0} | all-to-all | bytes 524288 | tf_op jit(solution)/shard_map/all_to_all | solution.py:40
  377.5 9.2 %all_to_all.205 = f32[8,4,2048]{2,0,1:T(8,128)S(1)} all-to-all(f32[8,4,2048]{2,0,1:T(8,128)S(1)} %bitcast.196), channel_id=1, replica_groups=mesh['site'=2,'wide'=32,'narrow'=4] {'narrow'}, dimensions={1} | all-to-all | bytes 524288 | tf_op jit(solution)/shard_map/all_to_all | solution.py:50
  386.7 5.3 fusion.4
  392.1 18.4 %reduce-scatter.13.cloned.1.call-done = f32[8,2,256]{2,0,1:T(8,128)} async-done(((f32[32,2,256]{2,0,1:T(8,128)}), f32[8,2,256]{2,0,1:T(8,128)}) %reduce-scatter.13.cloned.1.call-update) | async-done | bytes 16400 | tf_op jit(solution)/shard_map/reduce_scatter | solution.py:21
  411.3 63.2 %psum.45 = f32[8,2]{0,1:T(2,128)S(1)} all-reduce(f32[8,2]{0,1:T(2,128)S(1)} %multiply_reduce_fusion.2), channel_id=1, replica_groups=mesh['site'=2,'wide'=32,'narrow'=4] {'wide'}, use_global_device_ids=true, to_apply=%region_11.12 | all-reduce | flops 16 | bytes 128 | tf_op jit(solution)/shard_map/psum | solution.py:36
  475.5 24.8 %all_to_all.206 = f32[32,8,256]{2,1,0:T(8,128)S(1)} all-to-all(f32[32,8,256]{2,1,0:T(8,128)S(1)} %stack.15), channel_id=1, replica_groups=mesh['site'=2,'wide'=32,'narrow'=4] {'wide'}, dimensions={0} | all-to-all | bytes 524288 | tf_op jit(solution)/shard_map/all_to_all | solution.py:40
  500.2 9.2 %all_to_all.207 = f32[8,4,2048]{2,0,1:T(8,128)S(1)} all-to-all(f32[8,4,2048]{2,0,1:T(8,128)S(1)} %bitcast.197), channel_id=1, replica_groups=mesh['site'=2,'wide'=32,'narrow'=4] {'narrow'}, dimensions={1} | all-to-all | bytes 524288 | tf_op jit(solution)/shard_map/all_to_all | solution.py:50
  511.0 5.3 fusion
  516.3 18.4 %reduce-scatter.15.cloned.1.call-done = f32[8,2,256]{2,0,1:T(8,128)} async-done(((f32[32,2,256]{2,0,1:T(8,128)}), f32[8,2,256]{2,0,1:T(8,128)}) %reduce-scatter.15.cloned.1.call-update) | async-done | bytes 16400 | tf_op jit(solution)/shard_map/reduce_scatter | solution.py:21
  535.5 63.2 %psum.46 = f32[8,2]{0,1:T(2,128)S(1)} all-reduce(f32[8,2]{0,1:T(2,128)S(1)} %multiply_reduce_fusion.1), channel_id=1, replica_groups=mesh['site'=2,'wide'=32,'narrow'=4] {'wide'}, use_global_device_ids=true, to_apply=%region_14.15 | all-reduce | flops 16 | bytes 128 | tf_op jit(solution)/shard_map/psum | solution.py:36
  599.7 25.5 %all_to_all.208 = f32[32,8,256]{2,1,0:T(8,128)} all-to-all(f32[32,8,256]{2,1,0:T(8,128)S(1)} %stack.16), channel_id=1, replica_groups=mesh['site'=2,'wide'=32,'narrow'=4] {'wide'}, dimensions={0} | all-to-all | bytes 524288 | tf_op jit(solution)/shard_map/all_to_all | solution.py:40
  628.5 6.7 all-to-all-done.9
  639.1 5.3 fusion.3
  659.0 5.1 all-to-all-done.14
  667.9 6.0 reduce-scatter.17.cloned.1.call-done
  674.8 63.2 %psum.47 = f32[8,2]{0,1:T(2,128)S(1)} all-reduce(f32[8,2]{0,1:T(2,128)S(1)} %multiply_reduce_fusion), channel_id=1, replica_groups=mesh['site'=2,'wide'=32,'narrow'=4] {'wide'}, use_global_device_ids=true, to_apply=%region_17.18 | all-reduce | flops 16 | bytes 128 | tf_op jit(solution)/shard_map/psum | solution.py:36
  756.7 16.6 %all-to-all-start.10 = ((f32[32,8,256]{2,1,0:T(8,128)}), f32[32,8,256]{2,1,0:T(8,128)}, u32[]{:S(2)}, u32[]{:S(2)}) async-start(f32[32,8,256]{2,1,0:T(8,128)} %stack.17), calls=%async_computation.16 | async-start | bytes 524288 | tf_op jit(solution)/shard_map/all_to_all | solution.py:40
  773.8 9.3 %all-to-all-done.10 = f32[32,8,256]{2,1,0:T(8,128)} async-done(((f32[32,8,256]{2,1,0:T(8,128)}), f32[32,8,256]{2,1,0:T(8,128)}, u32[]{:S(2)}, u32[]{:S(2)}) %all-to-all-start.10) | async-done | bytes 262176 | tf_op jit(solution)/shard_map/all_to_all | solution.py:40
  787.0 6.1 all-to-all-done.11
  (88 shorter events, 67.1 us)
Async XLA Ops:
  7.2 255.1 %copy-start = (f32[32,1,2048]{2,1,0:T(1,128)S(1)}, f32[32,1,2048]{2,1,0:T(1,128)}, u32[]{:S(2)}) copy-start(f32[32,1,2048]{2,1,0:T(1,128)} %param.3) | copy-start | bytes 786436
  7.2 31.8 %reduce-scatter.7.cloned.1.call-start = ((), (), s32[]{:S(2)}) async-start(), calls=%async_computation.24 | async-start | bytes 81920 | tf_op jit(solution)/shard_map/reduce_scatter | solution.py:21
  12.7 149.0 %reduce-scatter.9.cloned.1.call-start = ((), (), s32[]{:S(2)}) async-start(), calls=%async_computation.25 | async-start | bytes 81920 | tf_op jit(solution)/shard_map/reduce_scatter | solution.py:21
  252.2 10.1 %all-to-all-start.3 = ((f32[8,4,2048]{2,0,1:T(8,128)}), f32[8,4,2048]{2,0,1:T(8,128)S(1)}, u32[]{:S(2)}, u32[]{:S(2)}) async-start(f32[8,4,2048]{2,0,1:T(8,128)} %bitcast.21), calls=%async_computation.5 | async-start | bytes 524288 | tf_op jit(solution)/shard_map/all_to_all | solution.py:50
  255.6 32.1 %reduce-scatter.11.cloned.1.call-start = ((), (), s32[]{:S(2)}) async-start(), calls=%async_computation.26 | async-start | bytes 81920 | tf_op jit(solution)/shard_map/reduce_scatter | solution.py:21
  262.3 1.6 collective-permute-start
  269.3 141.2 %reduce-scatter.13.cloned.1.call-start = ((), (), s32[]{:S(2)}) async-start(), calls=%async_computation.27 | async-start | bytes 81920 | tf_op jit(solution)/shard_map/reduce_scatter | solution.py:21
  392.0 142.7 %reduce-scatter.15.cloned.1.call-start = ((), (), s32[]{:S(2)}) async-start(), calls=%async_computation.28 | async-start | bytes 81920 | tf_op jit(solution)/shard_map/reduce_scatter | solution.py:21
  509.4 1.5 collective-permute-start.1
  625.1 10.1 %all-to-all-start.9 = ((f32[8,4,2048]{2,0,1:T(8,128)}), f32[8,4,2048]{2,0,1:T(8,128)S(1)}, u32[]{:S(2)}, u32[]{:S(2)}) async-start(f32[8,4,2048]{2,0,1:T(8,128)} %bitcast.50), calls=%async_computation.14 | async-start | bytes 524288 | tf_op jit(solution)/shard_map/all_to_all | solution.py:50
  635.8 8.6 %all-to-all-start.12 = ((f32[8,4,1]{0,2,1:T(1,128)}), f32[8,4,1]{0,2,1:T(1,128)S(1)}, u32[]{:S(2)}, u32[]{:S(2)}) async-start(f32[8,4,1]{0,2,1:T(1,128)} %broadcast_in_dim.96), calls=%async_computation.18 | async-start | bytes 4096 | tf_op jit(solution)/shard_map/all_to_all | solution.py:51
  644.9 10.0 %all-to-all-start.13 = ((f32[8,4,1]{0,2,1:T(1,128)}), f32[8,4,1]{0,2,1:T(1,128)S(1)}, u32[]{:S(2)}, u32[]{:S(2)}) async-start(f32[8,4,1]{0,2,1:T(1,128)} %broadcast_in_dim.97), calls=%async_computation.19 | async-start | bytes 4096 | tf_op jit(solution)/shard_map/all_to_all | solution.py:51
  649.7 24.2 %reduce-scatter.17.cloned.1.call-start = ((), (), s32[]{:S(2)}) async-start(), calls=%async_computation.29 | async-start | bytes 81920 | tf_op jit(solution)/shard_map/reduce_scatter | solution.py:21
  655.7 8.4 %all-to-all-start.14 = ((f32[8,4,1]{0,2,1:T(1,128)}), f32[8,4,1]{0,2,1:T(1,128)S(1)}, u32[]{:S(2)}, u32[]{:S(2)}) async-start(f32[8,4,1]{0,2,1:T(1,128)} %broadcast_in_dim.99), calls=%async_computation.20 | async-start | bytes 4096 | tf_op jit(solution)/shard_map/all_to_all | solution.py:51
  658.9 114.6 %collective-permute-start.2 = (f32[32]{0:T(128)S(1)}, f32[32]{0:T(128)S(1)}, u32[]{:S(2)}, u32[]{:S(2)}) collective-permute-start(f32[32]{0:T(128)S(1)} %select_n.137), channel_id=1, source_target_pairs={{0,128},{128,0},{1,129},{129,1},{2,130},{130,2},{3,131},{131,3},{4... | collective-permute-start | bytes 392 | tf_op jit(solution)/shard_map/ppermute | solution.py:14
  664.7 73.3 %all-to-all-start.15 = ((f32[8,4,1]{0,2,1:T(1,128)}), f32[8,4,1]{0,2,1:T(1,128)S(1)}, u32[]{:S(2)}, u32[]{:S(2)}) async-start(f32[8,4,1]{0,2,1:T(1,128)} %broadcast_in_dim.100), calls=%async_computation.21 | async-start | bytes 4096 | tf_op jit(solution)/shard_map/all_to_all | solution.py:51
  738.6 8.4 %all-to-all-start.16 = ((f32[8,4,1]{0,2,1:T(1,128)}), f32[8,4,1]{0,2,1:T(1,128)S(1)}, u32[]{:S(2)}, u32[]{:S(2)}) async-start(f32[8,4,1]{0,2,1:T(1,128)} %broadcast_in_dim.101), calls=%async_computation.22 | async-start | bytes 4096 | tf_op jit(solution)/shard_map/all_to_all | solution.py:51
  747.6 8.4 %all-to-all-start.17 = ((f32[8,4,1]{0,2,1:T(1,128)}), f32[8,4,1]{0,2,1:T(1,128)S(1)}, u32[]{:S(2)}, u32[]{:S(2)}) async-start(f32[8,4,1]{0,2,1:T(1,128)} %broadcast_in_dim.102), calls=%async_computation.23 | async-start | bytes 4096 | tf_op jit(solution)/shard_map/all_to_all | solution.py:51
  756.7 26.3 %all-to-all-start.10 = ((f32[32,8,256]{2,1,0:T(8,128)}), f32[32,8,256]{2,1,0:T(8,128)}, u32[]{:S(2)}, u32[]{:S(2)}) async-start(f32[32,8,256]{2,1,0:T(8,128)} %stack.17), calls=%async_computation.16 | async-start | bytes 524288 | tf_op jit(solution)/shard_map/all_to_all | solution.py:40
  773.4 13.0 %collective-permute-start.3 = (f32[32]{0:T(128)S(1)}, f32[32]{0:T(128)S(1)}, u32[]{:S(2)}, u32[]{:S(2)}) collective-permute-start(f32[32]{0:T(128)S(1)} %add_add_fusion), channel_id=1, source_target_pairs={{0,128},{128,0},{1,129},{129,1},{2,130},{130,2},{3,131},{131,3},{4... | collective-permute-start | bytes 392 | tf_op jit(solution)/shard_map/ppermute | solution.py:14
  783.1 10.1 %all-to-all-start.11 = ((f32[8,4,2048]{2,0,1:T(8,128)}), f32[8,4,2048]{2,0,1:T(8,128)S(1)}, u32[]{:S(2)}, u32[]{:S(2)}) async-start(f32[8,4,2048]{2,0,1:T(8,128)} %bitcast.59), calls=%async_computation.17 | async-start | bytes 524288 | tf_op jit(solution)/shard_map/all_to_all | solution.py:50
Sparse Core Ops, SparseCore 0:
  12.8 26.1 reduce-scatter.6
  143.4 18.2 reduce-scatter.8
  269.4 18.2 reduce-scatter.10
  392.1 18.2 reduce-scatter.12
  516.4 18.2 reduce-scatter.14
  653.2 20.6 reduce-scatter.16
